TPU v7x, 128 devices: a whole 4x4x4 slice. The times are simulated.
128 devices in a mesh: shard: 16 (over y, z), tensor: 4 (over x), section: 2 (over core).
Axes of the slice: x: 4, y: 4, z: 4, core: 2. Of those that a mesh axis runs over, the one named last changes fastest.
Arguments:
- attention_grads: float32 [16, 4, 768, 768], P('shard', 'section', 'tensor'), may hold values from -48 to 48
- feedforward_grads: float32 [16, 2, 3072, 768], P('shard', 'section', 'tensor'), may hold values from -48 to 48
- attention_errors: float32 [16, 4, 768, 768], P('shard', 'section', 'tensor'), may hold values from -3 to 3
- feedforward_errors: float32 [16, 2, 3072, 768], P('shard', 'section', 'tensor'), may hold values from -3 to 3
- attention_factor: float32 [4, 768, 32], P('section'), may hold values from -0.21875 to 0.21875
- feedforward_factor: float32 [2, 768, 32], P('section'), may hold values from -0.21875 to 0.21875
- attention_momentum: float32 [4, 768, 768], P('section', 'tensor', 'shard'), may hold values from -3 to 3
- feedforward_momentum: float32 [2, 3072, 768], P('section', 'tensor', 'shard'), may hold values from -3 to 3
- attention_master: float32 [4, 768, 768], P('section', 'tensor', 'shard'), may hold values from -3 to 3
- feedforward_master: float32 [2, 3072, 768], P('section', 'tensor', 'shard'), may hold values from -3 to 3
- gain_grads: float32 [16, 2, 768], P('shard', 'section', 'tensor'), may hold values from -6 to 6
- bias_grads: float32 [16, 12, 32], P('shard', 'tensor'), may hold values from -6 to 6
- gain_momentum: float32 [2, 768], P('section', 'tensor'), may hold values from -3 to 3
- gain_weight: float32 [2, 768], P('section', 'tensor'), may hold values from 0.5 to 1.5
- bias_momentum: float32 [12, 32], P('tensor'), may hold values from -3 to 3
- bias_weight: float32 [12, 32], P('tensor'), may hold values from -4 to 4
Outputs:
- attention_errors_new: float32 [16, 4, 768, 768], P('shard', 'section', 'tensor')
- feedforward_errors_new: float32 [16, 2, 3072, 768], P('shard', 'section', 'tensor')
- attention_factor_new: float32 [4, 768, 32], P('section')
- feedforward_factor_new: float32 [2, 768, 32], P('section')
- attention_momentum_new: float32 [4, 768, 768], P('section', 'tensor', 'shard')
- feedforward_momentum_new: float32 [2, 3072, 768], P('section', 'tensor', 'shard')
- attention_master_new: float32 [4, 768, 768], P('section', 'tensor', 'shard')
- feedforward_master_new: float32 [2, 3072, 768], P('section', 'tensor', 'shard')
- attention_fresh: bfloat16 [4, 768, 768], P('section', 'tensor')
- feedforward_fresh: bfloat16 [2, 3072, 768], P('section', 'tensor')
- gain_momentum_new: float32 [2, 768], P('section', 'tensor')
- gain_weight_new: float32 [2, 768], P('section', 'tensor')
- bias_momentum_new: float32 [12, 32], P('tensor')
- bias_weight_new: float32 [12, 32], P('tensor')
All inputs are finite; a program needn't handle non-finite values.
Results may differ from a plain program's by a relative error of at most 0.0004.
Values may be sent and summed in bfloat16 or wider, within the bound.
A program may use at most 64 MiB of HBM per device.

v0:
```python
import jax
import jax.numpy as jnp
from jax import lax
from jax.sharding import PartitionSpec as P

NS_STEPS = 5


exact_mode = lax.Precision.HIGHEST
learn_rate = 0.05
decay_rate = 0.9


def inverse_root(gram_matrix):
    identity = jnp.broadcast_to(
        jnp.eye(gram_matrix.shape[-1], dtype=jnp.float32), gram_matrix.shape
    )
    frob_scale = jnp.sqrt(jnp.sum(gram_matrix * gram_matrix, axis=(-2, -1), keepdims=True)) + 1e-06
    converge = gram_matrix / frob_scale
    inverse = identity
    for turn_index in range(NS_STEPS):
        middle = 0.5 * (3.0 * identity - jnp.matmul(inverse, converge, precision=exact_mode))
        converge, inverse = (
            jnp.matmul(converge, middle, precision=exact_mode),
            jnp.matmul(middle, inverse, precision=exact_mode),
        )
    return inverse / jnp.sqrt(frob_scale)


def left_terms(merged, factor):
    return jnp.einsum("rmij,mjk->mik", merged, factor, precision=exact_mode)


def row_gram(matrix):
    return jnp.einsum("mik,mil->mkl", matrix, matrix, precision=exact_mode)


def right_terms(merged, ortho):
    return jnp.einsum("rmij,mik->mjk", merged, ortho, precision=exact_mode)


def per_device(
    attention_grads,
    feedforward_grads,
    attention_errors,
    feedforward_errors,
    attention_factor,
    feedforward_factor,
    attention_momentum,
    feedforward_momentum,
    attention_master,
    feedforward_master,
    gain_grads,
    bias_grads,
    gain_momentum,
    gain_weight,
    bias_momentum,
    bias_weight,
):
    replicas = lax.axis_size("shard")
    column_width = attention_master.shape[2]
    column_start = lax.axis_index("shard") * column_width
    attention_base = attention_master - learn_rate * decay_rate * attention_momentum
    feedforward_base = feedforward_master - learn_rate * decay_rate * feedforward_momentum
    attention_merged = attention_grads + attention_errors
    feedforward_merged = feedforward_grads + feedforward_errors
    attention_part = left_terms(attention_merged, attention_factor)
    feedforward_part = left_terms(feedforward_merged, feedforward_factor)
    attention_power, feedforward_power = lax.psum((attention_part, feedforward_part), "shard")
    attention_gram, feedforward_gram = lax.psum(
        (row_gram(attention_power), row_gram(feedforward_power)), "tensor"
    )
    attention_ortho = jnp.matmul(
        attention_power, inverse_root(attention_gram), precision=exact_mode
    )
    feedforward_ortho = jnp.matmul(
        feedforward_power, inverse_root(feedforward_gram), precision=exact_mode
    )
    attention_back, feedforward_back = lax.psum(
        (
            right_terms(attention_merged, attention_ortho),
            right_terms(feedforward_merged, feedforward_ortho),
        ),
        ("shard", "tensor"),
    )
    attention_back = attention_back / replicas
    feedforward_back = feedforward_back / replicas
    attention_approx = jnp.einsum(
        "mik,mjk->mij", attention_ortho, attention_back, precision=exact_mode
    )
    feedforward_approx = jnp.einsum(
        "mik,mjk->mij", feedforward_ortho, feedforward_back, precision=exact_mode
    )
    attention_errors_new = attention_merged - attention_approx[None]
    feedforward_errors_new = feedforward_merged - feedforward_approx[None]
    attention_factor_new = jnp.matmul(
        attention_back, inverse_root(row_gram(attention_back)), precision=exact_mode
    )
    feedforward_factor_new = jnp.matmul(
        feedforward_back, inverse_root(row_gram(feedforward_back)), precision=exact_mode
    )
    attention_slice = lax.dynamic_slice_in_dim(attention_approx, column_start, column_width, 2)
    feedforward_slice = lax.dynamic_slice_in_dim(feedforward_approx, column_start, column_width, 2)
    attention_momentum_new = decay_rate * attention_momentum + attention_slice
    feedforward_momentum_new = decay_rate * feedforward_momentum + feedforward_slice
    attention_master_new = attention_base - learn_rate * attention_slice
    feedforward_master_new = feedforward_base - learn_rate * feedforward_slice
    attention_fresh, feedforward_fresh = (
        lax.all_gather(attention_master_new.astype(jnp.bfloat16), "shard", axis=2, tiled=True),
        lax.all_gather(feedforward_master_new.astype(jnp.bfloat16), "shard", axis=2, tiled=True),
    )
    gain_total, bias_total = lax.psum((gain_grads[0], bias_grads[0]), "shard")
    gain_momentum_new = decay_rate * gain_momentum + gain_total / replicas
    gain_weight_new = gain_weight - learn_rate * gain_momentum_new
    bias_momentum_new = decay_rate * bias_momentum + bias_total / replicas
    bias_weight_new = bias_weight - learn_rate * bias_momentum_new
    return (
        attention_errors_new,
        feedforward_errors_new,
        attention_factor_new,
        feedforward_factor_new,
        attention_momentum_new,
        feedforward_momentum_new,
        attention_master_new,
        feedforward_master_new,
        attention_fresh,
        feedforward_fresh,
        gain_momentum_new,
        gain_weight_new,
        bias_momentum_new,
        bias_weight_new,
    )


def solution(mesh):
    placed = (
        P("shard", "section", "tensor", None),
        P("shard", "section", "tensor", None),
        P("shard", "section", "tensor", None),
        P("shard", "section", "tensor", None),
        P("section", None, None),
        P("section", None, None),
        P("section", "tensor", "shard"),
        P("section", "tensor", "shard"),
        P("section", "tensor", "shard"),
        P("section", "tensor", "shard"),
        P("shard", "section", "tensor"),
        P("shard", "tensor", None),
        P("section", "tensor"),
        P("section", "tensor"),
        P("tensor", None),
        P("tensor", None),
    )
    return jax.shard_map(
        per_device,
        mesh=mesh,
        in_specs=placed,
        out_specs=(
            P("shard", "section", "tensor", None),
            P("shard", "section", "tensor", None),
            P("section", None, None),
            P("section", None, None),
            P("section", "tensor", "shard"),
            P("section", "tensor", "shard"),
            P("section", "tensor", "shard"),
            P("section", "tensor", "shard"),
            P("section", "tensor", None),
            P("section", "tensor", None),
            P("section", "tensor"),
            P("section", "tensor"),
            P("tensor", None),
            P("tensor", None),
        ),
        check_vma=False,
    )
```

profile of v0, /device:TPU:0, one launch (start us, length us, event | category | flops | bytes accessed | tf_op | source)
XLA Modules:
  0.0 321.8 jit_solution(5114528691584657770)
XLA Ops:
  7.3 3.2 copy.39
  10.5 2.0 copy.40
  12.4 2.7 add.70
  15.1 2.2 fusion.2
  17.4 1.8 add.68
  21.5 76.9 %all-reduce.1 = (f32[2,192,32]{1,2,0:T(8,128)S(1)}, f32[1,192]{1,0:T(1,128)S(1)}, f32[3,32]{1,0:T(4,128)S(1)}) all-reduce(f32[2,192,32]{1,2,0:T(8,128)S(1)} %fusion.6, f32[1,192]{1,0:T(1,128)S(1)} %bitcast.162, f32[3,32]{1,0:T(4,128)S(1)} %bitcast.161), channel_id=1, replica_groups=mesh['shard'=16,'tensor'=4,'section'=2] {'shard'}, use_global_device_ids=true, to_apply=%region_0.0 | all-reduce | flops 12576 | bytes 100608 | tf_op jit(solution)/shard_map/psum | solution.py:69
  98.6 3.7 %all-reduce.6.cloned.1.call-done = f32[768,32]{0,1:T(8,128)} async-done(((f32[768,32]{0,1:T(8,128)}), f32[768,32]{0,1:T(8,128)}) %all-reduce.6.cloned.1.call-update) | async-done | bytes 98320 | tf_op jit(solution)/shard_map/psum | solution.py:69
  103.6 17.4 %all-reduce.2 = (f32[2,32,32]{2,1,0:T(8,128)S(1)}, f32[1,32,32]{2,1,0:T(8,128)S(1)}) all-reduce(f32[2,32,32]{2,1,0:T(8,128)S(1)} %fusion.78, f32[1,32,32]{2,1,0:T(8,128)S(1)} %convolution_bitcast_fusion.1), channel_id=1, replica_groups=mesh['shard'=16,'tensor'=4,'section'=2] {'tensor'}, use_global_device_ids=true, to_apply=%region_1.0 | all-reduce | flops 3072 | bytes 24576 | tf_op jit(solution)/shard_map/psum | solution.py:70
  127.1 2.8 fusion.8
  130.5 1.4 fusion.4
  133.7 121.8 %all-reduce.8.cloned.1.call-done = (f32[2,768,32]{1,2,0:T(8,128)}, f32[1,768,32]{1,2,0:T(8,128)}) async-done(((f32[2,768,32]{1,2,0:T(8,128)}, f32[1,768,32]{1,2,0:T(8,128)}), (f32[2,768,32]{1,2,0:T(8,128)}, f32[1,768,32]{1,2,0:T(8,128)})) %all-reduce.8.cloned.1.call-update) | async-done | bytes 294928 | tf_op jit(solution)/shard_map/psum | solution.py:79
  255.5 1.8 multiply_reduce_fusion.2
  259.8 1.4 multiply_reduce_fusion
  264.2 4.5 %bitcast_subtract_fusion = (f32[1,1,768,768]{2,3,1,0:T(8,128)}, f32[768,768]{0,1:T(8,128)S(1)}) fusion(f32[1,1,768,768]{2,3,1,0:T(8,128)S(1)} %add.70, f32[768,32]{0,1:T(8,128)S(1)} %fusion.92, f32[1,768,32]{1,2,0:T(8,128)} %get-tuple-element.43), kind=kOutput, calls=%fused_computation | convolution fusion | flops 227106816 | bytes 7274496 | tf_op jit(solution)/shard_map/mik,mjk->mij/dot_general | solution.py:91
  268.7 2.6 bitcast_subtract_fusion.1
  272.1 1.9 fusion.77
  275.6 22.5 %all_gather.6 = bf16[2,192,768]{1,0,2:T(2,128)(2,1)S(1)} all-gather(bf16[2,192,48]{1,0,2:T(2,128)(2,1)} %copy.44), channel_id=1, replica_groups=mesh['shard'=16,'tensor'=4,'section'=2] {'shard'}, dimensions={2}, use_global_device_ids=true | all-gather | bytes 626688 | tf_op jit(solution)/shard_map/all_gather | solution.py:109
  298.2 2.0 copy.45
  300.1 1.7 copy.48
  301.8 1.7 copy.46
  303.5 1.7 copy.47
  305.2 1.8 convolution_bitcast_fusion
  311.0 1.9 all-gather.2.cloned.1.call-done
  312.9 2.4 copy.49
  (123 shorter events, 22.3 us)
Async XLA Ops:
  7.2 13.0 %copy-start = (f32[2,768,32]{1,2,0:T(8,128)S(1)}, f32[2,768,32]{1,2,0:T(8,128)}, u32[]{:S(2)}) copy-start(f32[2,768,32]{1,2,0:T(8,128)} %param.20) | copy-start | bytes 589828
  7.2 3.3 %copy-start.5 = (f32[1,1,768,768]{3,2,1,0:T(8,128)S(1)}, f32[1,1,768,768]{3,2,1,0:T(8,128)}, u32[]{:S(2)}) copy-start(f32[1,1,768,768]{3,2,1,0:T(8,128)} %param.19) | copy-start | bytes 7077892
  7.2 95.1 %all-reduce.6.cloned.1.call-start = ((), (), s32[]{:S(2)}) async-start(), calls=%async_computation | async-start | bytes 196608 | tf_op jit(solution)/shard_map/psum | solution.py:69
  12.4 2.7 copy-start.11
  15.1 2.3 copy-start.16
  17.3 238.1 %all-reduce.8.cloned.1.call-start = ((), (), s32[]{:S(2)}) async-start(), calls=%async_computation.2 | async-start | bytes 589824 | tf_op jit(solution)/shard_map/psum | solution.py:79
  17.4 4.0 %copy-start.17 = (f32[1,1,192]{2,1,0:T(1,128)S(1)}, f32[1,1,192]{2,1,0:T(1,128)}, u32[]{:S(2)}) copy-start(f32[1,1,192]{2,1,0:T(1,128)} %param.26) | copy-start | bytes 2308
  19.2 1.0 copy-start.1
  102.3 24.4 %copy-start.7 = (f32[768,32]{0,1:T(8,128)S(1)}, f32[768,32]{0,1:T(8,128)}, u32[]{:S(2)}) copy-start(f32[768,32]{0,1:T(8,128)} %all-reduce.6.cloned.1.call-done) | copy-start | bytes 294916
  124.1 6.4 %copy-start.2 = (f32[1,2,192,768]{3,2,1,0:T(8,128)S(1)}, f32[1,2,192,768]{3,2,1,0:T(8,128)}, u32[]{:S(2)}) copy-start(f32[1,2,192,768]{3,2,1,0:T(8,128)} %copy-done.1) | copy-start | bytes 3538948
  127.0 5.2 %copy-start.18 = (f32[1,192]{1,0:T(1,128)S(1)}, f32[1,192]{1,0:T(1,128)}, u32[]{:S(2)}) copy-start(f32[1,192]{1,0:T(1,128)} %param.29) | copy-start | bytes 2308
  127.0 5.2 %copy-start.19 = (f32[1,192]{1,0:T(1,128)S(1)}, f32[1,192]{1,0:T(1,128)}, u32[]{:S(2)}) copy-start(f32[1,192]{1,0:T(1,128)} %param.28) | copy-start | bytes 2308
  127.0 5.8 %copy-start.12 = (f32[2,192,48]{1,2,0:T(8,128)S(1)}, f32[2,192,48]{1,2,0:T(8,128)}, u32[]{:S(2)}) copy-start(f32[2,192,48]{1,2,0:T(8,128)} %param.22) | copy-start | bytes 221188
  127.0 5.9 %copy-start.13 = (f32[2,192,48]{1,2,0:T(8,128)S(1)}, f32[2,192,48]{1,2,0:T(8,128)}, u32[]{:S(2)}) copy-start(f32[2,192,48]{1,2,0:T(8,128)} %param.24) | copy-start | bytes 221188
  127.0 6.0 %copy-start.14 = (f32[3,32]{1,0:T(4,128)S(1)}, f32[3,32]{1,0:T(4,128)}, u32[]{:S(2)}) copy-start(f32[3,32]{1,0:T(4,128)} %param.31) | copy-start | bytes 1156
  127.1 6.0 %copy-start.15 = (f32[3,32]{1,0:T(4,128)S(1)}, f32[3,32]{1,0:T(4,128)}, u32[]{:S(2)}) copy-start(f32[3,32]{1,0:T(4,128)} %param.30) | copy-start | bytes 1156
  132.0 181.0 %all-gather.2.cloned.1.call-start = ((), (), s32[]{:S(2)}) async-start(), calls=%async_computation.1 | async-start | bytes 1253376 | tf_op jit(solution)/shard_map/all_gather | solution.py:110
  264.2 4.5 %copy-start.3 = (f32[1,2,192,768]{3,2,1,0:T(8,128)S(1)}, f32[1,2,192,768]{3,2,1,0:T(8,128)}, u32[]{:S(2)}) copy-start(f32[1,2,192,768]{3,2,1,0:T(8,128)} %copy-done.1) | copy-start | bytes 3538948
  264.2 4.5 %copy-start.6 = (f32[2,768,32]{1,2,0:T(8,128)S(1)}, f32[2,768,32]{1,2,0:T(8,128)}, u32[]{:S(2)}) copy-start(f32[2,768,32]{1,2,0:T(8,128)} %get-tuple-element.42) | copy-start | bytes 589828
  268.7 2.6 copy-start.9
  268.7 2.6 copy-start.10
  271.3 26.9 %copy-start.4 = (f32[1,1,768,768]{2,3,1,0:T(8,128)S(1)}, f32[1,1,768,768]{2,3,1,0:T(8,128)}, u32[]{:S(2)}) copy-start(f32[1,1,768,768]{2,3,1,0:T(8,128)} %get-tuple-element.65) | copy-start | bytes 7077892
  300.1 8.8 %copy-start.8 = (f32[2,32,32]{2,1,0:T(8,128)S(1)}, f32[2,32,32]{2,1,0:T(8,128)}, u32[]{:S(2)}) copy-start(f32[2,32,32]{2,1,0:T(8,128)} %fusion.93) | copy-start | bytes 24580
  300.1 9.6 %copy-start.20 = (f32[2]{0:T(128)S(1)}, f32[2]{0:T(128)}, u32[]{:S(2)}) copy-start(f32[2]{0:T(128)} %get-tuple-element.59) | copy-start | bytes 28
Sparse Core Ops, SparseCore 0:
  17.5 84.7 all-reduce.5
  132.1 123.3 all-reduce.7
  272.2 40.6 all-gather.1
where the time goes:
time: 322 us
  waiting for transfers between devices  128 us (40%)
  blocking collectives  117 us (36%)
  matrix products  35.2 us (11%)
  local copies, waits for them, and re-layouts  16.6 us (5%)
  between operations  15.8 us (5%)
  other arithmetic  9.61 us (3%)
    psum x1, waiting for transfers between devices, per_device(): lax.psum((right_terms(attention_merged, attention_ortho), right_terms(fee...  122 us
    psum x1, blocking collectives, per_device(): lax.psum((attention_part, feedforward_part), 'shard')  76.9 us
    all_gather x1, blocking collectives, per_device(): lax.all_gather(attention_master_new.astype(jnp.bfloat16), 'shard', axis=2...  22.5 us
    psum x1, blocking collectives, per_device(): lax.psum((row_gram(attention_power), row_gram(feedforward_power)), 'tensor')  17.4 us
    unnamed x52, local copies, waits for them, and re-layouts  15.9 us
  transfers between devices with their start and end apart: 3, of which 3 were waited for; matrix products, arithmetic and copies ran while one was open for 6% of the time, Pallas kernels for 0%

commit v1 on v0

v1 whole, which is shorter than its diff:
```python
import jax
import jax.numpy as jnp
from jax import lax
from jax.experimental import pallas as pl
from jax.experimental.pallas import tpu as pltpu
from jax.sharding import PartitionSpec as P

NS_STEPS = 5
RANK = 32
MESH = pl.DeviceIdType.MESH

exact_mode = lax.Precision.HIGHEST
learn_rate = 0.05
decay_rate = 0.9


def dot(a, b, dims):
    return lax.dot_general(
        a, b, ((dims[:1], dims[1:]), ((), ())), precision=exact_mode,
        preferred_element_type=jnp.float32,
    )


def block_mask(size):
    row = lax.broadcasted_iota(jnp.int32, (size, size), 0)
    col = lax.broadcasted_iota(jnp.int32, (size, size), 1)
    return (row >> 5) == (col >> 5), row == col


def inverse_root(gram):
    size = gram.shape[0]
    _, diagonal = block_mask(size)
    identity = jnp.where(diagonal, 1.0, 0.0).astype(jnp.float32)
    squares = jnp.sum(gram * gram, axis=1, keepdims=True)
    scale = jnp.concatenate(
        [
            jnp.broadcast_to(
                jnp.sqrt(jnp.sum(squares[at : at + RANK], axis=0, keepdims=True)) + 1e-06,
                (RANK, 1),
            )
            for at in range(0, size, RANK)
        ],
        axis=0,
    )
    converge = gram / scale
    inverse = None
    for turn in range(NS_STEPS):
        product = converge if turn == 0 else dot(inverse, converge, (1, 0))
        middle = 0.5 * (3.0 * identity - product)
        inverse = middle if turn == 0 else dot(middle, inverse, (1, 0))
        if turn < NS_STEPS - 1:
            converge = dot(converge, middle, (1, 0))
    return inverse / jnp.sqrt(scale)


def remote(src, dst, send_sem, recv_sem, device):
    return pltpu.make_async_remote_copy(
        src_ref=src, dst_ref=dst, send_sem=send_sem, recv_sem=recv_sem,
        device_id=device, device_id_type=MESH,
    )


CHUNKS = 12


def exchange_kernel(
    att_grads, ff_grads, att_errors, ff_errors, factor, base, small,
    ortho_out, back_out, factor_out, small_out, base_out,
    merged, errors, part, part_slots, power, gram_slots, back_part, back_slots,
    back_pieces, back, small_slots,
    load_sem, base_sem, part_send, part_recv, power_send, power_recv, gram_send, gram_recv,
    bpart_send, bpart_recv, piece_send, piece_recv, back_send, back_recv,
    small_send, small_recv, first_send, first_recv, second_send, second_recv,
):
    me = lax.axis_index("shard")
    my_tensor = lax.axis_index("tensor")
    my_y, my_z = me // 4, me % 4
    rows = (384, 768)

    def shard_peer(d):
        return lax.rem(me + d, 16)

    def shard_source(d):
        return lax.rem(me + 16 - d, 16)

    loads = []
    for at, (g, e) in enumerate(((att_grads, att_errors), (ff_grads, ff_errors))):
        for piece in range(1 if at == 0 else 2):
            source = pl.ds(piece * 384, 384)
            target = pl.ds((at + piece) * 384, 384)
            n = at + piece
            loads.append((
                pltpu.make_async_copy(g.at[source], merged.at[target], load_sem.at[n, 0]),
                pltpu.make_async_copy(e.at[source], errors.at[target], load_sem.at[n, 1]),
            ))
    for g, e in loads:
        g.start()
        e.start()
    own_base = pltpu.make_async_copy(base, base_out.at[my_y, my_z], base_sem)
    own_base.start()

    barrier = pltpu.get_barrier_semaphore()

    @pl.loop(1, 16)
    def _(d):
        pl.semaphore_signal(barrier, inc=1, device_id={"shard": shard_peer(d)}, device_id_type=MESH)

    for d in range(1, 4):
        pl.semaphore_signal(
            barrier, inc=1, device_id={"tensor": lax.rem(my_tensor + d, 4)}, device_id_type=MESH
        )

    lane = lax.broadcasted_iota(jnp.int32, (RANK, 384), 1)
    for n in range(3):
        for copy in loads[n]:
            copy.wait()
        at = pl.ds(n * 384, 384)
        total = merged[at] + errors[at]
        merged[at] = total
        if n == 0:
            both = dot(total, factor[0:64], (1, 1)).T
            left = jnp.where(lane < 192, both[0:32], both[32:64])
        else:
            left = dot(total, factor[64:96], (1, 1)).T
        part[4 * n : 4 * n + 4] = left.reshape(4, 8, 384)
    small_slots[me] = small[...]

    pl.semaphore_wait(barrier, 18)

    def part_copy(d):
        return remote(
            part.at[lax.rem(shard_peer(d), CHUNKS)], part_slots.at[d], part_send.at[d],
            part_recv.at[d], {"shard": shard_peer(d)},
        )

    def small_copy(d):
        return remote(
            small_slots.at[me], small_slots.at[me], small_send.at[d], small_recv.at[d],
            {"shard": shard_peer(d)},
        )

    @pl.loop(1, 16)
    def _(d):
        @pl.when(shard_peer(d) < CHUNKS)
        def _():
            part_copy(d).start()

    def first_copy(half, d):
        if half == 0:
            device = {"shard": lax.rem(my_y + d, 4) * 4 + my_z}
        else:
            device = {"shard": my_y * 4 + lax.rem(my_z + d, 4)}
        return remote(
            base.at[half], base_out.at[my_y, my_z, half], first_send.at[half, d],
            first_recv.at[half, d], device,
        )

    def second_copy(half, d):
        if half == 0:
            device = {"shard": my_y * 4 + lax.rem(my_z + d, 4)}
            piece = base_out.at[:, my_z, 0]
        else:
            device = {"shard": lax.rem(my_y + d, 4) * 4 + my_z}
            piece = base_out.at[my_y, :, 1]
        return remote(piece, piece, second_send.at[half, d], second_recv.at[half, d], device)

    for half in range(2):
        for d in range(1, 4):
            first_copy(half, d).start()

    @pl.loop(1, 16)
    def _(d):
        small_copy(d).start()

    def power_copy(d):
        return remote(
            power.at[me], power.at[me], power_send.at[d], power_recv.at[d],
            {"shard": shard_peer(d)},
        )

    @pl.when(me < CHUNKS)
    def _():
        @pl.loop(1, 16)
        def _(d):
            part_copy(d).wait_recv()

        total = part[me]
        for d in range(1, 16):
            total += part_slots[d]
        power[me] = total

        @pl.loop(1, 16)
        def _(d):
            power_copy(d).start()

    own_base.wait()
    for half in range(2):
        for d in range(1, 4):
            first_copy(half, d).wait_recv()
    for half in range(2):
        for d in range(1, 4):
            second_copy(half, d).start()

    @pl.loop(1, 16)
    def _(d):
        @pl.when(shard_source(d) < CHUNKS)
        def _():
            remote(
                power.at[0], power.at[0], power_send.at[d], power_recv.at[d],
                {"shard": shard_peer(d)},
            ).wait_recv()

    zeros = jnp.zeros((RANK, 384), jnp.float32)
    spread = []
    for n in range(3):
        left = power[4 * n : 4 * n + 4].reshape(RANK, 384)
        if n == 0:
            spread.append(
                jnp.concatenate(
                    [jnp.where(lane < 192, left, 0.0), jnp.where(lane < 192, 0.0, left), zeros], axis=0
                )
            )
        else:
            spread.append(jnp.concatenate([zeros, zeros, left], axis=0))
    blocks, _ = block_mask(96)
    gram = dot(spread[0], spread[0], (1, 1))
    gram += dot(spread[1], spread[1], (1, 1))
    gram += dot(spread[2], spread[2], (1, 1))
    gram_slots[my_tensor] = gram[0:32] + gram[32:64] + gram[64:96]

    def gram_copy(d):
        return remote(
            gram_slots.at[my_tensor], gram_slots.at[my_tensor], gram_send.at[d], gram_recv.at[d],
            {"tensor": lax.rem(my_tensor + d, 4)},
        )

    for d in range(1, 4):
        gram_copy(d).start()
    for d in range(1, 4):
        gram_copy(d).wait_recv()
    total = (gram_slots[0] + gram_slots[1]) + (gram_slots[2] + gram_slots[3])
    root = inverse_root(jnp.where(blocks, jnp.concatenate([total, total, total], axis=0), 0.0))

    right = None
    for n in range(3):
        ortho = dot(root, spread[n], (0, 0))
        ortho_out[:, n * 384 : n * 384 + 384] = ortho
        term = dot(ortho, merged[n * 384 : n * 384 + 384], (1, 0))
        right = term if right is None else right + term
    back_part[...] = right.reshape(CHUNKS, 8, 768)

    def bpart_copy(d):
        return remote(
            back_part.at[lax.rem(shard_peer(d), CHUNKS)], back_slots.at[d], bpart_send.at[d],
            bpart_recv.at[d], {"shard": shard_peer(d)},
        )

    def piece_copy(d):
        return remote(
            back_pieces.at[my_tensor], back_pieces.at[my_tensor], piece_send.at[d],
            piece_recv.at[d], {"tensor": lax.rem(my_tensor + d, 4)},
        )

    def back_copy(d):
        return remote(
            back.at[me], back.at[me], back_send.at[d], back_recv.at[d],
            {"shard": shard_peer(d)},
        )

    @pl.loop(1, 16)
    def _(d):
        @pl.when(shard_peer(d) < CHUNKS)
        def _():
            bpart_copy(d).start()

    @pl.when(me < CHUNKS)
    def _():
        @pl.loop(1, 16)
        def _(d):
            bpart_copy(d).wait_recv()

        total = back_part[me]
        for d in range(1, 16):
            total += back_slots[d]
        back_pieces[my_tensor] = total
        for d in range(1, 4):
            piece_copy(d).start()
        for d in range(1, 4):
            piece_copy(d).wait_recv()
        total = (back_pieces[0] + back_pieces[1]) + (back_pieces[2] + back_pieces[3])
        back[me] = total * (1.0 / 16.0)

        @pl.loop(1, 16)
        def _(d):
            back_copy(d).start()

    @pl.loop(1, 16)
    def _(d):
        @pl.when(shard_source(d) < CHUNKS)
        def _():
            remote(
                back.at[0], back.at[0], back_send.at[d], back_recv.at[d],
                {"shard": shard_peer(d)},
            ).wait_recv()

    total = back[...].reshape(96, 768)
    back_out[...] = total
    root = inverse_root(jnp.where(blocks, dot(total, total, (1, 1)), 0.0))
    factor_out[...] = dot(root, total, (0, 0))

    @pl.loop(1, 16)
    def _(d):
        small_copy(d).wait_recv()

    total = small_slots[0]
    for n in range(1, 16):
        total += small_slots[n]
    small_out[...] = total

    for half in range(2):
        for d in range(1, 4):
            second_copy(half, d).wait_recv()

    @pl.loop(1, 16)
    def _(d):
        small_copy(d).wait_send()

        @pl.when(shard_peer(d) < CHUNKS)
        def _():
            part_copy(d).wait_send()
            bpart_copy(d).wait_send()

    @pl.when(me < CHUNKS)
    def _():
        @pl.loop(1, 16)
        def _(d):
            power_copy(d).wait_send()
            back_copy(d).wait_send()

        for d in range(1, 4):
            piece_copy(d).wait_send()

    for d in range(1, 4):
        gram_copy(d).wait_send()
        for half in range(2):
            first_copy(half, d).wait_send()
            second_copy(half, d).wait_send()


def exchange(att_grads, ff_grads, att_errors, ff_errors, factor, base, small):
    any_spec = pl.BlockSpec(memory_space=pl.ANY)
    vmem_spec = pl.BlockSpec(memory_space=pltpu.VMEM)
    dma = pltpu.SemaphoreType.DMA
    f32 = jnp.float32
    return pl.pallas_call(
        exchange_kernel,
        out_shape=(
            jax.ShapeDtypeStruct((96, 1152), f32),
            jax.ShapeDtypeStruct((96, 768), f32),
            jax.ShapeDtypeStruct((96, 768), f32),
            jax.ShapeDtypeStruct((8, 128), f32),
            jax.ShapeDtypeStruct((4, 4, 2, 24, 1152), f32),
        ),
        in_specs=[any_spec] * 4 + [vmem_spec] * 3,
        out_specs=(vmem_spec, vmem_spec, vmem_spec, vmem_spec, any_spec),
        scratch_shapes=[
            pltpu.VMEM((1152, 768), f32),
            pltpu.VMEM((1152, 768), f32),
            pltpu.VMEM((12, 8, 384), f32),
            pltpu.VMEM((16, 8, 384), f32),
            pltpu.VMEM((12, 8, 384), f32),
            pltpu.VMEM((4, 32, 96), f32),
            pltpu.VMEM((12, 8, 768), f32),
            pltpu.VMEM((16, 8, 768), f32),
            pltpu.VMEM((4, 8, 768), f32),
            pltpu.VMEM((12, 8, 768), f32),
            pltpu.VMEM((16, 8, 128), f32),
            dma((3, 2)),
            dma,
        ]
        + [dma((16,))] * 4
        + [dma((4,))] * 2
        + [dma((16,))] * 2
        + [dma((4,))] * 2
        + [dma((16,))] * 4
        + [dma((2, 4))] * 4,
        compiler_params=pltpu.CompilerParams(
            collective_id=0, has_side_effects=True, vmem_limit_bytes=40 * 1024 * 1024
        ),
        name="exchange",
    )(att_grads, ff_grads, att_errors, ff_errors, factor, base, small)


def per_device(
    attention_grads,
    feedforward_grads,
    attention_errors,
    feedforward_errors,
    attention_factor,
    feedforward_factor,
    attention_momentum,
    feedforward_momentum,
    attention_master,
    feedforward_master,
    gain_grads,
    bias_grads,
    gain_momentum,
    gain_weight,
    bias_momentum,
    bias_weight,
):
    replicas = 16
    start = lax.axis_index("shard") * 48
    att_grads = attention_grads.reshape(384, 768)
    ff_grads = feedforward_grads.reshape(768, 768)
    att_errors = attention_errors.reshape(384, 768)
    ff_errors = feedforward_errors.reshape(768, 768)
    factor = jnp.concatenate([attention_factor, feedforward_factor], axis=0)
    factor = jnp.swapaxes(factor, 1, 2).reshape(96, 768)

    def columns(att, ff):
        return jnp.concatenate([att[0].T, att[1].T, ff[0].T], axis=1)

    momentum = columns(attention_momentum, feedforward_momentum)
    master = columns(attention_master, feedforward_master)
    base = master - learn_rate * decay_rate * momentum
    small = jnp.concatenate([gain_grads.reshape(2, 96), bias_grads.reshape(1, 96)], axis=0)
    small = jnp.pad(small, ((0, 5), (0, 32)))
    ortho, back, factor_new, small_total, base_full = exchange(
        att_grads, ff_grads, att_errors, ff_errors, factor, base.reshape(2, 24, 1152), small
    )

    approx = dot(ortho, back, (0, 0))
    att_errors_new = att_grads + att_errors - approx[:384]
    ff_errors_new = ff_grads + ff_errors - approx[384:]
    own = dot(lax.dynamic_slice_in_dim(back, start, 48, 1), ortho, (0, 0))
    momentum_new = decay_rate * momentum + own
    master_new = base - learn_rate * own
    fresh = base_full.reshape(768, 1152).T - learn_rate * approx
    fresh = fresh.astype(jnp.bfloat16)

    def split(values):
        return (
            jnp.stack([values[:, :192].T, values[:, 192:384].T]),
            values[:, 384:].T[None],
        )

    att_momentum_new, ff_momentum_new = split(momentum_new)
    att_master_new, ff_master_new = split(master_new)
    factor_new = jnp.swapaxes(factor_new.reshape(3, 32, 768), 1, 2)
    gain_total = small_total[0:2, :96].reshape(1, 192)
    bias_total = small_total[2:3, :96].reshape(3, 32)
    gain_momentum_new = decay_rate * gain_momentum + gain_total / replicas
    gain_weight_new = gain_weight - learn_rate * gain_momentum_new
    bias_momentum_new = decay_rate * bias_momentum + bias_total / replicas
    bias_weight_new = bias_weight - learn_rate * bias_momentum_new
    return (
        att_errors_new.reshape(1, 2, 192, 768),
        ff_errors_new.reshape(1, 1, 768, 768),
        factor_new[:2],
        factor_new[2:],
        att_momentum_new,
        ff_momentum_new,
        att_master_new,
        ff_master_new,
        fresh[:384].reshape(2, 192, 768),
        fresh[384:].reshape(1, 768, 768),
        gain_momentum_new,
        gain_weight_new,
        bias_momentum_new,
        bias_weight_new,
    )


def solution(mesh):
    placed = (
        P("shard", "section", "tensor", None),
        P("shard", "section", "tensor", None),
        P("shard", "section", "tensor", None),
        P("shard", "section", "tensor", None),
        P("section", None, None),
        P("section", None, None),
        P("section", "tensor", "shard"),
        P("section", "tensor", "shard"),
        P("section", "tensor", "shard"),
        P("section", "tensor", "shard"),
        P("shard", "section", "tensor"),
        P("shard", "tensor", None),
        P("section", "tensor"),
        P("section", "tensor"),
        P("tensor", None),
        P("tensor", None),
    )
    return jax.shard_map(
        per_device,
        mesh=mesh,
        in_specs=placed,
        out_specs=(
            P("shard", "section", "tensor", None),
            P("shard", "section", "tensor", None),
            P("section", None, None),
            P("section", None, None),
            P("section", "tensor", "shard"),
            P("section", "tensor", "shard"),
            P("section", "tensor", "shard"),
            P("section", "tensor", "shard"),
            P("section", "tensor", None),
            P("section", "tensor", None),
            P("section", "tensor"),
            P("section", "tensor"),
            P("tensor", None),
            P("tensor", None),
        ),
        check_vma=False,
    )
```

time: 322 us -> 104 us (0.32)
  waiting for transfers between devices: 128 us -> 0 us
  blocking collectives: 117 us -> 0 us
  Pallas kernels: 0 us -> 64.1 us
  matrix products: 35.2 us -> 6.7 us
  between operations: 15.8 us -> 0.79 us
  local copies, waits for them, and re-layouts: 16.6 us -> 24.9 us
    psum x2 -> x0, waiting for transfers between devices: 126 us -> none  [the longest x1 122 us: per_device(): lax.psum((right_terms(attention_merged, attention_ortho), right_terms(fee...]
    psum x2 -> x0, blocking collectives: 94.3 us -> none  [the longest x1 76.9 us: per_device(): lax.psum((attention_part, feedforward_part), 'shard')]
    pallas_call x0 -> x1, Pallas kernels: none -> 64.1 us  [exchange(): pl.pallas_call(exchange_kernel, out_shape=(jax.ShapeDtypeStruct((96, 1152...]
    dot_general x70 -> x2, matrix products: 35.2 us -> 6.7 us  [dot(): lax.dot_general(a, b, ((dims[:1], dims[1:]), ((), ())), precision=exact_m...]
    all_gather x1 -> x0, blocking collectives: 22.5 us -> none  [per_device(): lax.all_gather(attention_master_new.astype(jnp.bfloat16), 'shard', axis=2...]
    unnamed x52 -> x39, local copies, waits for them, and re-layouts: 15.9 us -> 8.27 us
    reshape x0 -> x4, local copies, waits for them, and re-layouts: none -> 6.48 us  [the longest x1 5.22 us: per_device(): fresh = base_full.reshape(768, 1152).T - learn_rate * approx]
    add x2 -> x0, other arithmetic: 4.47 us -> none  [the longest x1 2.7 us: per_device(): feedforward_merged = feedforward_grads + feedforward_errors]
  transfers between devices with their start and end apart: 3 -> 0, of which waited for: 3 -> 0; matrix products, arithmetic and copies ran while one was open for 6% -> 0% of each run, Pallas kernels for 0% -> 0%
where the time goes in v1:
time: 104 us
  Pallas kernels  64.1 us (62%)
  local copies, waits for them, and re-layouts  24.9 us (24%)
  other arithmetic  7.27 us (7%)
  matrix products  6.7 us (6%)
    pallas_call x1, Pallas kernels, exchange(): pl.pallas_call(exchange_kernel, out_shape=(jax.ShapeDtypeStruct((96, 1152...  64.1 us
    unnamed x39, local copies, waits for them, and re-layouts  8.27 us
    dot_general x2, matrix products, dot(): lax.dot_general(a, b, ((dims[:1], dims[1:]), ((), ())), precision=exact_m...  6.7 us
    reshape x1, local copies, waits for them, and re-layouts, per_device(): fresh = base_full.reshape(768, 1152).T - learn_rate * approx  5.22 us
    concatenate x4, local copies, waits for them, and re-layouts, columns(): return jnp.concatenate([att[0].T, att[1].T, ff[0].T], axis=1)  3.95 us
    transpose x2, local copies, waits for them, and re-layouts, columns(): return jnp.concatenate([att[0].T, att[1].T, ff[0].T], axis=1)  3.07 us

profile of v1, /device:TPU:0, one launch (start us, length us, event | category | flops | bytes accessed | tf_op | source)
XLA Modules:
  0.0 103.8 jit_solution(3768770339508152451)
XLA Ops:
  0.7 1.6 %slice_bitcast_fusion.9 = (f32[48,192]{1,0:T(8,128)S(1)}, f32[48,192]{1,0:T(8,128)}, f32[1,192,48]{1,2,0:T(8,128)S(1)}, f32[1,192,48]{1,2,0:T(8,128)S(1)}) fusion(f32[2,192,48]{1,2,0:T(8,128)} %param.24), kind=kLoop, calls=%fused_computation.32 | loop fusion | bytes 221184 | tf_op jit(solution)/shard_map/transpose | solution.py:422
  2.3 1.0 concatenate.34
  3.3 1.5 %slice_bitcast_fusion.7 = (f32[48,192]{1,0:T(8,128)}, f32[48,192]{1,0:T(8,128)}, f32[1,192,48]{1,2,0:T(8,128)S(1)}, f32[1,192,48]{1,2,0:T(8,128)S(1)}) fusion(f32[2,192,48]{1,2,0:T(8,128)} %param.22), kind=kLoop, calls=%fused_computation.30 | loop fusion | bytes 221184 | tf_op jit(solution)/shard_map/transpose | solution.py:422
  4.8 1.0 concatenate.38
  5.8 1.0 pad_maximum_fusion
  7.3 0.7 reduce.8
  8.2 1.7 %copy-done.1 = f32[1,1,768,768]{3,2,1,0:T(8,128)S(1)} copy-done((f32[1,1,768,768]{3,2,1,0:T(8,128)S(1)}, f32[1,1,768,768]{3,2,1,0:T(8,128)}, u32[]{:S(2)}) %copy-start.1) | copy-done | bytes 2359320
  9.9 1.3 %copy-done.3 = f32[1,2,192,768]{3,2,1,0:T(8,128)S(1)} copy-done((f32[1,2,192,768]{3,2,1,0:T(8,128)S(1)}, f32[1,2,192,768]{3,2,1,0:T(8,128)}, u32[]{:S(2)}) %copy-start.3) | copy-done | bytes 1179672
  11.1 1.3 %copy-done.5 = f32[1,2,192,768]{3,2,1,0:T(8,128)S(1)} copy-done((f32[1,2,192,768]{3,2,1,0:T(8,128)S(1)}, f32[1,2,192,768]{3,2,1,0:T(8,128)}, u32[]{:S(2)}) %copy-start.5) | copy-done | bytes 1179672
  12.4 64.1 %exchange.1 = (f32[96,1152]{1,0:T(8,128)S(1)}, f32[96,768]{1,0:T(8,128)S(1)}, f32[96,768]{1,0:T(8,128)S(1)}, f32[8,128]{1,0:T(8,128)S(1)}, f32[4,4,2,24,1152]{4,3,2,1,0:T(8,128)S(1)}) custom-call(f32[384,768]{1,0:T(8,128)S(1)} %bitcast.88, f32[768,768]{1,0:T(8,128)S(1)} %bitcast.86, f32[384,768]{1,0:T(8,128)S(1)} %bitcast.89, f32[768,768]{1,0:T(8,128)S(1)} %bitcast.87, ...), custom_call_target="tpu_custom_call" | custom-call | tf_op jit(solution)/shard_map/exchange/pallas_call | solution.py:355
  76.5 1.8 %copy-done.7 = f32[4,4,2,24,1152]{4,3,2,1,0:T(8,128)} copy-done((f32[4,4,2,24,1152]{4,3,2,1,0:T(8,128)}, f32[4,4,2,24,1152]{4,3,2,1,0:T(8,128)S(1)}, u32[]{:S(2)}) %copy-start.7) | copy-done | bytes 3538968
  78.3 0.7 copy-done.8
  79.0 0.7 copy-done.10
  79.7 0.9 concatenate.40
  80.6 1.0 concatenate.41
  81.6 1.4 %multiply_subtract_fusion = (f32[48,1152]{1,0:T(8,128)S(1)}, f32[48,1152]{1,0:T(8,128)S(1)}) fusion(f32[48,1152]{1,0:T(8,128)S(1)} %concatenate.41, f32[48,1152]{1,0:T(8,128)S(1)} %concatenate.40, f32[96,1152]{1,0:T(8,128)S(1)} %get-tuple-element.19, f32[96,768]{1,0:T(8,128)} %copy-done.8, s32[]{:T(128)S(6)} %select_n.3), kind=kOutput, calls=%fused_computation.7 | convolution fusion | flops 64032768 | bytes 1376260 | tf_op jit(solution)/shard_map/dot_general | solution.py:18
  83.8 0.7 slice_bitcast_fusion.1
  85.2 5.2 %copy.30 = f32[768,1152]{0,1:T(8,128)} copy(f32[768,1152]{1,0:T(8,128)} %bitcast.90) | data formatting | bytes 7077888 | tf_op jit(solution)/shard_map/reshape | solution.py:439
  90.4 5.3 %fusion = (bf16[1152,768]{1,0:T(8,128)(2,1)S(1)}, f32[1152,768]{1,0:T(8,128)S(1)}) fusion(f32[768,1152]{0,1:T(8,128)} %copy.30, f32[96,1152]{1,0:T(8,128)S(1)} %get-tuple-element.19, f32[96,768]{1,0:T(8,128)S(1)} %copy-done.9), kind=kOutput, calls=%fused_computation.1 | convolution fusion | flops 1021870080 | bytes 9584640 | tf_op jit(solution)/shard_map/dot_general | solution.py:18
  95.8 1.8 %fusion.1 = f32[1,1,768,768]{3,2,1,0:T(8,128)} fusion(f32[1152,768]{1,0:T(8,128)S(1)} %get-tuple-element.43, f32[1,1,768,768]{3,2,1,0:T(8,128)S(1)} %copy-done.2, f32[1,1,768,768]{3,2,1,0:T(8,128)S(1)} %copy-done), kind=kLoop, calls=%fused_computation.3 | loop fusion | flops 1179648 | bytes 9437184 | tf_op jit(solution)/shard_map/reshape | solution.py:459
  97.9 1.2 %slice_subtract_fusion.1 = f32[384,768]{1,0:T(8,128)} fusion(f32[1152,768]{1,0:T(8,128)S(1)} %get-tuple-element.43, f32[1,2,192,768]{3,2,1,0:T(8,128)S(1)} %copy-done.6, f32[1,2,192,768]{3,2,1,0:T(8,128)S(1)} %copy-done.4), kind=kLoop, calls=%fused_computation.5 | loop fusion | flops 589824 | bytes 4718592 | tf_op jit(solution)/shard_map/sub | solution.py:434
  99.2 1.1 %slice_bitcast_fusion = bf16[1,768,768]{2,1,0:T(8,128)(2,1)} fusion(bf16[1152,768]{1,0:T(8,128)(2,1)S(1)} %get-tuple-element.42), kind=kLoop, calls=%fused_computation.4 | loop fusion | bytes 2359296 | tf_op jit(solution)/shard_map/reshape | solution.py:467
  100.3 0.9 slice.82
  102.5 0.7 slice.74
  (48 shorter events, 4.5 us)
Async XLA Ops:
  0.6 6.7 %copy-start.18 = (f32[1,1,192]{2,1,0:T(1,128)S(1)}, f32[1,1,192]{2,1,0:T(1,128)}, u32[]{:S(2)}) copy-start(f32[1,1,192]{2,1,0:T(1,128)} %param.26) | copy-start | bytes 2308
  0.7 7.4 %copy-start.15 = (f32[1,3,32]{2,0,1:T(1,128)S(1)}, f32[1,3,32]{2,0,1:T(1,128)}, u32[]{:S(2)}) copy-start(f32[1,3,32]{2,0,1:T(1,128)} %param.27) | copy-start | bytes 1156
  0.7 7.5 %copy-start = (f32[1,1,768,768]{3,2,1,0:T(8,128)S(1)}, f32[1,1,768,768]{3,2,1,0:T(8,128)}, u32[]{:S(2)}) copy-start(f32[1,1,768,768]{3,2,1,0:T(8,128)} %param.17) | copy-start | bytes 7077892
  8.2 1.7 %copy-start.1 = (f32[1,1,768,768]{3,2,1,0:T(8,128)S(1)}, f32[1,1,768,768]{3,2,1,0:T(8,128)}, u32[]{:S(2)}) copy-start(f32[1,1,768,768]{3,2,1,0:T(8,128)} %param.19) | copy-start | bytes 7077892
  9.9 1.3 %copy-start.3 = (f32[1,2,192,768]{3,2,1,0:T(8,128)S(1)}, f32[1,2,192,768]{3,2,1,0:T(8,128)}, u32[]{:S(2)}) copy-start(f32[1,2,192,768]{3,2,1,0:T(8,128)} %param.16) | copy-start | bytes 3538948
  11.1 1.3 %copy-start.5 = (f32[1,2,192,768]{3,2,1,0:T(8,128)S(1)}, f32[1,2,192,768]{3,2,1,0:T(8,128)}, u32[]{:S(2)}) copy-start(f32[1,2,192,768]{3,2,1,0:T(8,128)} %param.18) | copy-start | bytes 3538948
  12.4 67.3 %copy-start.12 = (f32[1,768,48]{1,2,0:T(8,128)S(1)}, f32[1,768,48]{1,2,0:T(8,128)}, u32[]{:S(2)}) copy-start(f32[1,768,48]{1,2,0:T(8,128)} %param.23) | copy-start | bytes 442372
  76.5 1.8 %copy-start.7 = (f32[4,4,2,24,1152]{4,3,2,1,0:T(8,128)}, f32[4,4,2,24,1152]{4,3,2,1,0:T(8,128)S(1)}, u32[]{:S(2)}) copy-start(f32[4,4,2,24,1152]{4,3,2,1,0:T(8,128)S(1)} %get-tuple-element.22) | copy-start | bytes 10616836
  78.3 0.7 copy-start.8
  79.0 0.7 copy-start.10
  85.2 5.2 %copy-start.9 = (f32[96,768]{1,0:T(8,128)S(1)}, f32[96,768]{1,0:T(8,128)}, u32[]{:S(2)}) copy-start(f32[96,768]{1,0:T(8,128)} %copy-done.8) | copy-start | bytes 884740
  90.4 5.3 %copy-start.2 = (f32[1,1,768,768]{3,2,1,0:T(8,128)S(1)}, f32[1,1,768,768]{3,2,1,0:T(8,128)}, u32[]{:S(2)}) copy-start(f32[1,1,768,768]{3,2,1,0:T(8,128)} %param.19) | copy-start | bytes 7077892
  95.7 1.9 %copy-start.4 = (f32[1,2,192,768]{3,2,1,0:T(8,128)S(1)}, f32[1,2,192,768]{3,2,1,0:T(8,128)}, u32[]{:S(2)}) copy-start(f32[1,2,192,768]{3,2,1,0:T(8,128)} %param.16) | copy-start | bytes 3538948
  95.7 2.2 %copy-start.6 = (f32[1,2,192,768]{3,2,1,0:T(8,128)S(1)}, f32[1,2,192,768]{3,2,1,0:T(8,128)}, u32[]{:S(2)}) copy-start(f32[1,2,192,768]{3,2,1,0:T(8,128)} %param.18) | copy-start | bytes 3538948
  99.1 2.1 %copy-start.13 = (f32[3,32]{1,0:T(4,128)S(1)}, f32[3,32]{1,0:T(4,128)}, u32[]{:S(2)}) copy-start(f32[3,32]{1,0:T(4,128)} %param.31) | copy-start | bytes 1156
  99.1 2.1 %copy-start.14 = (f32[3,32]{1,0:T(4,128)S(1)}, f32[3,32]{1,0:T(4,128)}, u32[]{:S(2)}) copy-start(f32[3,32]{1,0:T(4,128)} %param.30) | copy-start | bytes 1156
  99.1 2.8 %copy-start.16 = (f32[1,192]{1,0:T(1,128)S(1)}, f32[1,192]{1,0:T(1,128)}, u32[]{:S(2)}) copy-start(f32[1,192]{1,0:T(1,128)} %param.29) | copy-start | bytes 2308
  99.2 2.8 %copy-start.17 = (f32[1,192]{1,0:T(1,128)S(1)}, f32[1,192]{1,0:T(1,128)}, u32[]{:S(2)}) copy-start(f32[1,192]{1,0:T(1,128)} %param.28) | copy-start | bytes 2308
  99.2 3.3 %copy-start.11 = (f32[96,768]{1,0:T(8,128)S(1)}, f32[96,768]{1,0:T(8,128)}, u32[]{:S(2)}) copy-start(f32[96,768]{1,0:T(8,128)} %copy-done.10) | copy-start | bytes 884740

commit v2 on v1

--- a/solution.py
+++ b/solution.py
@@ -64,11 +64,12 @@
 
 
 def exchange_kernel(
-    att_grads, ff_grads, att_errors, ff_errors, factor, base, small,
+    att_grads, ff_grads, att_errors, ff_errors, att_factor_in, ff_factor_in,
+    att_momentum_in, ff_momentum_in, att_master_in, ff_master_in, gain, bias,
     ortho_out, back_out, factor_out, small_out, base_out,
-    merged, errors, part, part_slots, power, gram_slots, back_part, back_slots,
+    merged, errors, factor, att_momentum, ff_momentum, att_master, ff_master, base, part, part_slots, power, gram_slots, back_part, back_slots,
     back_pieces, back, small_slots,
-    load_sem, base_sem, part_send, part_recv, power_send, power_recv, gram_send, gram_recv,
+    load_sem, state_sem, base_sem, part_send, part_recv, power_send, power_recv, gram_send, gram_recv,
     bpart_send, bpart_recv, piece_send, piece_recv, back_send, back_recv,
     small_send, small_recv, first_send, first_recv, second_send, second_recv,
 ):
@@ -93,11 +94,19 @@
                 pltpu.make_async_copy(g.at[source], merged.at[target], load_sem.at[n, 0]),
                 pltpu.make_async_copy(e.at[source], errors.at[target], load_sem.at[n, 1]),
             ))
+    states = [
+        pltpu.make_async_copy(source, target, state_sem.at[n])
+        for n, (source, target) in enumerate((
+            (att_momentum_in, att_momentum), (ff_momentum_in, ff_momentum),
+            (att_master_in, att_master), (ff_master_in, ff_master),
+            (att_factor_in, factor.at[pl.ds(0, 64)]), (ff_factor_in, factor.at[pl.ds(64, 32)]),
+        ))
+    ]
+    for copy in states:
+        copy.start()
     for g, e in loads:
         g.start()
         e.start()
-    own_base = pltpu.make_async_copy(base, base_out.at[my_y, my_z], base_sem)
-    own_base.start()
 
     barrier = pltpu.get_barrier_semaphore()
 
@@ -109,6 +118,50 @@
         pl.semaphore_signal(
             barrier, inc=1, device_id={"tensor": lax.rem(my_tensor + d, 4)}, device_id_type=MESH
         )
+
+    def part_copy(d):
+        return remote(
+            part.at[lax.rem(shard_peer(d), CHUNKS)], part_slots.at[d], part_send.at[d],
+            part_recv.at[d], {"shard": shard_peer(d)},
+        )
+
+    def small_copy(d):
+        return remote(
+            small_slots.at[me], small_slots.at[me], small_send.at[d], small_recv.at[d],
+            {"shard": shard_peer(d)},
+        )
+
+    def first_copy(half, d):
+        if half == 0:
+            device = {"shard": lax.rem(my_y + d, 4) * 4 + my_z}
+        else:
+            device = {"shard": my_y * 4 + lax.rem(my_z + d, 4)}
+        return remote(
+            base.at[half], base_out.at[my_y, my_z, half], first_send.at[half, d],
+            first_recv.at[half, d], device,
+        )
+
+    def second_copy(half, d):
+        if half == 0:
+            device = {"shard": my_y * 4 + lax.rem(my_z + d, 4)}
+            piece = base_out.at[:, my_z, 0]
+        else:
+            device = {"shard": lax.rem(my_y + d, 4) * 4 + my_z}
+            piece = base_out.at[my_y, :, 1]
+        return remote(piece, piece, second_send.at[half, d], second_recv.at[half, d], device)
+
+    for copy in states:
+        copy.wait()
+    step = learn_rate * decay_rate
+    for half in range(2):
+        at = slice(24 * half, 24 * half + 24)
+        att = att_master[:, at] - step * att_momentum[:, at]
+        base[half, :, 0:384] = jnp.concatenate([att[0], att[1]], axis=1)
+        base[half, :, 384:1152] = ff_master[at] - step * ff_momentum[at]
+    own_base = pltpu.make_async_copy(base, base_out.at[my_y, my_z], base_sem)
+    own_base.start()
+    small_slots[me, 0:1, 0:192] = gain[...]
+    small_slots[me, 1:4, 0:32] = bias[...]
 
     lane = lax.broadcasted_iota(jnp.int32, (RANK, 384), 1)
     for n in range(3):
@@ -123,50 +176,19 @@
         else:
             left = dot(total, factor[64:96], (1, 1)).T
         part[4 * n : 4 * n + 4] = left.reshape(4, 8, 384)
-    small_slots[me] = small[...]
-
-    pl.semaphore_wait(barrier, 18)
-
-    def part_copy(d):
-        return remote(
-            part.at[lax.rem(shard_peer(d), CHUNKS)], part_slots.at[d], part_send.at[d],
-            part_recv.at[d], {"shard": shard_peer(d)},
-        )
-
-    def small_copy(d):
-        return remote(
-            small_slots.at[me], small_slots.at[me], small_send.at[d], small_recv.at[d],
-            {"shard": shard_peer(d)},
-        )
-
-    @pl.loop(1, 16)
-    def _(d):
-        @pl.when(shard_peer(d) < CHUNKS)
-        def _():
-            part_copy(d).start()
-
-    def first_copy(half, d):
-        if half == 0:
-            device = {"shard": lax.rem(my_y + d, 4) * 4 + my_z}
-        else:
-            device = {"shard": my_y * 4 + lax.rem(my_z + d, 4)}
-        return remote(
-            base.at[half], base_out.at[my_y, my_z, half], first_send.at[half, d],
-            first_recv.at[half, d], device,
-        )
-
-    def second_copy(half, d):
-        if half == 0:
-            device = {"shard": my_y * 4 + lax.rem(my_z + d, 4)}
-            piece = base_out.at[:, my_z, 0]
-        else:
-            device = {"shard": lax.rem(my_y + d, 4) * 4 + my_z}
-            piece = base_out.at[my_y, :, 1]
-        return remote(piece, piece, second_send.at[half, d], second_recv.at[half, d], device)
-
-    for half in range(2):
-        for d in range(1, 4):
-            first_copy(half, d).start()
+        if n == 0:
+            pl.semaphore_wait(barrier, 18)
+
+        @pl.loop(1, 16)
+        def _(d):
+            @pl.when((shard_peer(d) >= 4 * n) & (shard_peer(d) < 4 * n + 4))
+            def _():
+                part_copy(d).start()
+
+        if n == 0:
+            for half in range(2):
+                for d in range(1, 4):
+                    first_copy(half, d).start()
 
     @pl.loop(1, 16)
     def _(d):
@@ -347,7 +369,7 @@
             second_copy(half, d).wait_send()
 
 
-def exchange(att_grads, ff_grads, att_errors, ff_errors, factor, base, small):
+def exchange(*operands):
     any_spec = pl.BlockSpec(memory_space=pl.ANY)
     vmem_spec = pl.BlockSpec(memory_space=pltpu.VMEM)
     dma = pltpu.SemaphoreType.DMA
@@ -358,14 +380,20 @@
             jax.ShapeDtypeStruct((96, 1152), f32),
             jax.ShapeDtypeStruct((96, 768), f32),
             jax.ShapeDtypeStruct((96, 768), f32),
-            jax.ShapeDtypeStruct((8, 128), f32),
+            jax.ShapeDtypeStruct((8, 256), f32),
             jax.ShapeDtypeStruct((4, 4, 2, 24, 1152), f32),
         ),
-        in_specs=[any_spec] * 4 + [vmem_spec] * 3,
+        in_specs=[any_spec] * 10 + [vmem_spec] * 2,
         out_specs=(vmem_spec, vmem_spec, vmem_spec, vmem_spec, any_spec),
         scratch_shapes=[
             pltpu.VMEM((1152, 768), f32),
             pltpu.VMEM((1152, 768), f32),
+            pltpu.VMEM((96, 768), f32),
+            pltpu.VMEM((2, 48, 192), f32),
+            pltpu.VMEM((48, 768), f32),
+            pltpu.VMEM((2, 48, 192), f32),
+            pltpu.VMEM((48, 768), f32),
+            pltpu.VMEM((2, 24, 1152), f32),
             pltpu.VMEM((12, 8, 384), f32),
             pltpu.VMEM((16, 8, 384), f32),
             pltpu.VMEM((12, 8, 384), f32),
@@ -374,8 +402,9 @@
             pltpu.VMEM((16, 8, 768), f32),
             pltpu.VMEM((4, 8, 768), f32),
             pltpu.VMEM((12, 8, 768), f32),
-            pltpu.VMEM((16, 8, 128), f32),
+            pltpu.VMEM((16, 8, 256), f32),
             dma((3, 2)),
+            dma((6,)),
             dma,
         ]
         + [dma((16,))] * 4
@@ -384,11 +413,91 @@
         + [dma((4,))] * 2
         + [dma((16,))] * 4
         + [dma((2, 4))] * 4,
-        compiler_params=pltpu.CompilerParams(
-            collective_id=0, has_side_effects=True, vmem_limit_bytes=40 * 1024 * 1024
-        ),
+        compiler_params=pltpu.CompilerParams(collective_id=0, has_side_effects=True),
         name="exchange",
-    )(att_grads, ff_grads, att_errors, ff_errors, factor, base, small)
+    )(*operands)
+
+
+ROWS = 128
+
+
+def update_kernel(
+    att_grads, att_errors, ff_grads, ff_errors, ortho, back, base,
+    att_momentum, ff_momentum, att_master, ff_master, small,
+    gain_momentum, gain_weight, bias_momentum, bias_weight,
+    att_errors_out, ff_errors_out, att_fresh_out, ff_fresh_out,
+    att_momentum_out, ff_momentum_out, att_master_out, ff_master_out,
+    gain_momentum_out, gain_weight_out, bias_momentum_out, bias_weight_out,
+):
+    n = pl.program_id(0)
+    at = pl.ds(pl.multiple_of(n * ROWS, ROWS), ROWS)
+    approx = dot(ortho[:, at], back[...], (0, 0))
+    fresh = (base[...].T - learn_rate * approx).astype(jnp.bfloat16)
+
+    @pl.when(n < 3)
+    def _():
+        att_errors_out[...] = att_grads[...] + att_errors[...] - approx
+        att_fresh_out[...] = fresh
+
+    @pl.when(n >= 3)
+    def _():
+        ff_errors_out[...] = ff_grads[...] + ff_errors[...] - approx
+        ff_fresh_out[...] = fresh
+
+    @pl.when(n == 0)
+    def _():
+        shard = lax.axis_index("shard")
+        own_back = pltpu.roll(back[...], lax.rem(768 - 48 * shard, 768), 1)[:, 0:128]
+        own = dot(own_back, ortho[...], (0, 0))[0:48]
+        step = learn_rate * decay_rate
+        att_own = own[:, 0:384]
+        for m in range(2):
+            piece = (att_own if m == 0 else pltpu.roll(att_own, 192, 1))[:, 0:192]
+            att_momentum_out[m] = decay_rate * att_momentum[m] + piece
+            att_master_out[m] = att_master[m] - step * att_momentum[m] - learn_rate * piece
+        piece = own[:, 384:1152]
+        ff_momentum_out[...] = decay_rate * ff_momentum[...] + piece
+        ff_master_out[...] = ff_master[...] - step * ff_momentum[...] - learn_rate * piece
+        gain = decay_rate * gain_momentum[...] + small[0:1, 0:192] * (1.0 / 16.0)
+        gain_momentum_out[...] = gain
+        gain_weight_out[...] = gain_weight[...] - learn_rate * gain
+        bias = decay_rate * bias_momentum[...] + small[1:4, 0:32] * (1.0 / 16.0)
+        bias_momentum_out[...] = bias
+        bias_weight_out[...] = bias_weight[...] - learn_rate * bias
+
+
+def update(*operands):
+    def att_block(n):
+        return jnp.minimum(n, 2), 0
+
+    def ff_block(n):
+        return jnp.maximum(n - 3, 0), 0
+
+    def whole(*shape):
+        return pl.BlockSpec(shape, lambda n: (0,) * len(shape))
+
+    att = pl.BlockSpec((ROWS, 768), att_block)
+    ff = pl.BlockSpec((ROWS, 768), ff_block)
+    states = [whole(2, 48, 192), whole(48, 768)]
+    vectors = [whole(1, 192)] * 2 + [whole(3, 32)] * 2
+    shapes = [
+        ((384, 768), jnp.float32), ((768, 768), jnp.float32),
+        ((384, 768), jnp.bfloat16), ((768, 768), jnp.bfloat16),
+        ((2, 48, 192), jnp.float32), ((48, 768), jnp.float32),
+        ((2, 48, 192), jnp.float32), ((48, 768), jnp.float32),
+        ((1, 192), jnp.float32), ((1, 192), jnp.float32),
+        ((3, 32), jnp.float32), ((3, 32), jnp.float32),
+    ]
+    return pl.pallas_call(
+        update_kernel,
+        grid=(1152 // ROWS,),
+        out_shape=[jax.ShapeDtypeStruct(*shape) for shape in shapes],
+        in_specs=[att, att, ff, ff, whole(96, 1152), whole(96, 768)]
+        + [pl.BlockSpec((768, ROWS), lambda n: (0, n))]
+        + states + states + [whole(8, 256)] + vectors,
+        out_specs=[att, ff, att, ff] + states + states + vectors,
+        name="update",
+    )(*operands)
 
 
 def per_device(
@@ -409,66 +518,39 @@
     bias_momentum,
     bias_weight,
 ):
-    replicas = 16
-    start = lax.axis_index("shard") * 48
     att_grads = attention_grads.reshape(384, 768)
     ff_grads = feedforward_grads.reshape(768, 768)
     att_errors = attention_errors.reshape(384, 768)
     ff_errors = feedforward_errors.reshape(768, 768)
-    factor = jnp.concatenate([attention_factor, feedforward_factor], axis=0)
-    factor = jnp.swapaxes(factor, 1, 2).reshape(96, 768)
-
-    def columns(att, ff):
-        return jnp.concatenate([att[0].T, att[1].T, ff[0].T], axis=1)
-
-    momentum = columns(attention_momentum, feedforward_momentum)
-    master = columns(attention_master, feedforward_master)
-    base = master - learn_rate * decay_rate * momentum
-    small = jnp.concatenate([gain_grads.reshape(2, 96), bias_grads.reshape(1, 96)], axis=0)
-    small = jnp.pad(small, ((0, 5), (0, 32)))
+    states = (
+        jnp.swapaxes(attention_momentum, 1, 2), feedforward_momentum[0].T,
+        jnp.swapaxes(attention_master, 1, 2), feedforward_master[0].T,
+    )
     ortho, back, factor_new, small_total, base_full = exchange(
-        att_grads, ff_grads, att_errors, ff_errors, factor, base.reshape(2, 24, 1152), small
-    )
-
-    approx = dot(ortho, back, (0, 0))
-    att_errors_new = att_grads + att_errors - approx[:384]
-    ff_errors_new = ff_grads + ff_errors - approx[384:]
-    own = dot(lax.dynamic_slice_in_dim(back, start, 48, 1), ortho, (0, 0))
-    momentum_new = decay_rate * momentum + own
-    master_new = base - learn_rate * own
-    fresh = base_full.reshape(768, 1152).T - learn_rate * approx
-    fresh = fresh.astype(jnp.bfloat16)
-
-    def split(values):
-        return (
-            jnp.stack([values[:, :192].T, values[:, 192:384].T]),
-            values[:, 384:].T[None],
-        )
-
-    att_momentum_new, ff_momentum_new = split(momentum_new)
-    att_master_new, ff_master_new = split(master_new)
+        att_grads, ff_grads, att_errors, ff_errors,
+        jnp.swapaxes(attention_factor, 1, 2).reshape(64, 768), feedforward_factor[0].T,
+        *states, gain_grads.reshape(1, 192), bias_grads.reshape(3, 32),
+    )
+    (
+        att_errors_new, ff_errors_new, att_fresh, ff_fresh,
+        att_momentum_new, ff_momentum_new, att_master_new, ff_master_new, *vectors,
+    ) = update(
+        att_grads, att_errors, ff_grads, ff_errors, ortho, back, base_full.reshape(768, 1152),
+        *states, small_total, gain_momentum, gain_weight, bias_momentum, bias_weight,
+    )
     factor_new = jnp.swapaxes(factor_new.reshape(3, 32, 768), 1, 2)
-    gain_total = small_total[0:2, :96].reshape(1, 192)
-    bias_total = small_total[2:3, :96].reshape(3, 32)
-    gain_momentum_new = decay_rate * gain_momentum + gain_total / replicas
-    gain_weight_new = gain_weight - learn_rate * gain_momentum_new
-    bias_momentum_new = decay_rate * bias_momentum + bias_total / replicas
-    bias_weight_new = bias_weight - learn_rate * bias_momentum_new
     return (
         att_errors_new.reshape(1, 2, 192, 768),
         ff_errors_new.reshape(1, 1, 768, 768),
         factor_new[:2],
         factor_new[2:],
-        att_momentum_new,
-        ff_momentum_new,
-        att_master_new,
-        ff_master_new,
-        fresh[:384].reshape(2, 192, 768),
-        fresh[384:].reshape(1, 768, 768),
-        gain_momentum_new,
-        gain_weight_new,
-        bias_momentum_new,
-        bias_weight_new,
+        jnp.swapaxes(att_momentum_new, 1, 2),
+        ff_momentum_new.T[None],
+        jnp.swapaxes(att_master_new, 1, 2),
+        ff_master_new.T[None],
+        att_fresh.reshape(2, 192, 768),
+        ff_fresh.reshape(1, 768, 768),
+        *vectors,
     )
 
 

time: 104 us -> 82.6 us (0.79)
  local copies, waits for them, and re-layouts: 24.9 us -> 4.42 us
  Pallas kernels: 64.1 us -> 77.2 us
  other arithmetic: 7.27 us -> 0 us
  matrix products: 6.7 us -> 0 us
    pallas_call x0 -> x1, Pallas kernels: none -> 13 us  [update(): pl.pallas_call(update_kernel, grid=(1152 // ROWS,), out_shape=[jax.ShapeD...]
    unnamed x39 -> x1, local copies, waits for them, and re-layouts: 8.27 us -> 1.26 us
    dot_general x2 -> x0, matrix products: 6.7 us -> none  [dot(): lax.dot_general(a, b, ((dims[:1], dims[1:]), ((), ())), precision=exact_m...]
    reshape x4 -> x0, local copies, waits for them, and re-layouts: 6.48 us -> none  [the longest x1 5.22 us: per_device(): fresh = base_full.reshape(768, 1152).T - learn_rate * approx]
    concatenate x4 -> x0, local copies, waits for them, and re-layouts: 3.95 us -> none  [columns(): return jnp.concatenate([att[0].T, att[1].T, ff[0].T], axis=1)]
    transpose x2 -> x0, local copies, waits for them, and re-layouts: 3.07 us -> none  [columns(): return jnp.concatenate([att[0].T, att[1].T, ff[0].T], axis=1)]
    sub x4 -> x0, other arithmetic: 2.41 us -> none  [the longest x1 1.21 us: per_device(): att_errors_new = att_grads + att_errors - approx[:384]]
    reshape x1 -> x0, other arithmetic: 1.85 us -> none  [per_device(): ff_errors_new.reshape(1, 1, 768, 768)]
where the time goes in v2:
time: 82.6 us; the launch traced here: 82.2 us
  Pallas kernels  77.2 us (93%)
  local copies, waits for them, and re-layouts  4.42 us (5%)
    pallas_call x1, Pallas kernels, exchange(): pl.pallas_call(exchange_kernel, out_shape=(jax.ShapeDtypeStruct((96, 1152...  64.2 us
    pallas_call x1, Pallas kernels, update(): pl.pallas_call(update_kernel, grid=(1152 // ROWS,), out_shape=[jax.ShapeD...  13 us

profile of v2, /device:TPU:0, one launch (start us, length us, event | category | flops | bytes accessed | tf_op | source)
XLA Modules:
  0.0 82.2 jit_solution(157268002055026325)
XLA Ops:
  0.6 1.3 %copy.32 = f32[1,3,32]{2,1,0:T(4,128)} copy(f32[1,3,32]{2,0,1:T(1,128)} %param.27) | data formatting | bytes 768
  1.9 64.2 %exchange.1 = (f32[96,1152]{1,0:T(8,128)}, f32[96,768]{1,0:T(8,128)}, f32[96,768]{1,0:T(8,128)}, f32[8,256]{1,0:T(8,128)}, f32[4,4,2,24,1152]{4,3,2,1,0:T(8,128)}) custom-call(f32[384,768]{1,0:T(8,128)} %bitcast.42, f32[768,768]{1,0:T(8,128)} %bitcast.38, f32[384,768]{1,0:T(8,128)} %bitcast.44, f32[768,768]{1,0:T(8,128)} %bitcast.40, f32[64,768]{1,0:T(8,128)} %bitcast.57, ...), custom_call_target="tpu_custom_call" | custom-call | tf_op jit(solution)/shard_map/exchange/pallas_call | solution.py:377
  66.1 1.5 %slice.9 = f32[1,768,32]{1,2,0:T(8,128)} slice(f32[3,768,32]{1,2,0:T(8,128)} %bitcast.55), slice={[2:3], [0:768], [0:32]} | slice | bytes 196608 | tf_op jit(solution)/shard_map/slice | solution.py:546
  67.7 1.6 %slice.8 = f32[2,768,32]{1,2,0:T(8,128)} slice(f32[3,768,32]{1,2,0:T(8,128)} %bitcast.56), slice={[0:2], [0:768], [0:32]} | slice | bytes 393216 | tf_op jit(solution)/shard_map/slice | solution.py:545
  69.3 13.0 %update.1 = (f32[384,768]{1,0:T(8,128)}, f32[768,768]{1,0:T(8,128)}, bf16[384,768]{1,0:T(8,128)(2,1)}, bf16[768,768]{1,0:T(8,128)(2,1)}, f32[2,48,192]{2,1,0:T(8...) custom-call(f32[384,768]{1,0:T(8,128)} %bitcast.43, ...), custom_call_target="tpu_custom_call" | custom-call | tf_op jit(solution)/shard_map/update/pallas_call | solution.py:491

commit v3 on v2

--- a/solution.py
+++ b/solution.py
@@ -18,6 +18,17 @@
     return lax.dot_general(
         a, b, ((dims[:1], dims[1:]), ((), ())), precision=exact_mode,
         preferred_element_type=jnp.float32,
+    )
+
+
+def halves(value):
+    high = value.astype(jnp.bfloat16)
+    return high, (value - high.astype(jnp.float32)).astype(jnp.bfloat16)
+
+
+def short_dot(a, b, dims):
+    return lax.dot_general(
+        a, b, ((dims[:1], dims[1:]), ((), ())), preferred_element_type=jnp.float32
     )
 
 
@@ -67,7 +78,7 @@
     att_grads, ff_grads, att_errors, ff_errors, att_factor_in, ff_factor_in,
     att_momentum_in, ff_momentum_in, att_master_in, ff_master_in, gain, bias,
     ortho_out, back_out, factor_out, small_out, base_out,
-    merged, errors, factor, att_momentum, ff_momentum, att_master, ff_master, base, part, part_slots, power, gram_slots, back_part, back_slots,
+    merged, errors, merged_high, merged_low, factor, att_momentum, ff_momentum, att_master, ff_master, base, part, part_slots, power, gram_slots, back_part, back_slots,
     back_pieces, back, small_slots,
     load_sem, state_sem, base_sem, part_send, part_recv, power_send, power_recv, gram_send, gram_recv,
     bpart_send, bpart_recv, piece_send, piece_recv, back_send, back_recv,
@@ -161,20 +172,24 @@
     own_base = pltpu.make_async_copy(base, base_out.at[my_y, my_z], base_sem)
     own_base.start()
     small_slots[me, 0:1, 0:192] = gain[...]
-    small_slots[me, 1:4, 0:32] = bias[...]
+    small_slots[me, 1:4, 0:32] = bias[...].reshape(3, 32)
 
     lane = lax.broadcasted_iota(jnp.int32, (RANK, 384), 1)
     for n in range(3):
         for copy in loads[n]:
             copy.wait()
         at = pl.ds(n * 384, 384)
-        total = merged[at] + errors[at]
-        merged[at] = total
+        high, low = halves(merged[at] + errors[at])
+        merged_high[at] = high
+        merged_low[at] = low
         if n == 0:
-            both = dot(total, factor[0:64], (1, 1)).T
-            left = jnp.where(lane < 192, both[0:32], both[32:64])
+            size, (factor_high, factor_low) = 64, halves(factor[0:64])
         else:
-            left = dot(total, factor[64:96], (1, 1)).T
+            size, (factor_high, factor_low) = 32, halves(factor[64:96])
+        both = short_dot(high, jnp.concatenate([factor_high, factor_low], axis=0), (1, 1))
+        left = (both[:, 0:size] + both[:, size : 2 * size] + short_dot(low, factor_high, (1, 1))).T
+        if n == 0:
+            left = jnp.where(lane < 192, left[0:32], left[32:64])
         part[4 * n : 4 * n + 4] = left.reshape(4, 8, 384)
         if n == 0:
             pl.semaphore_wait(barrier, 18)
@@ -263,13 +278,20 @@
     total = (gram_slots[0] + gram_slots[1]) + (gram_slots[2] + gram_slots[3])
     root = inverse_root(jnp.where(blocks, jnp.concatenate([total, total, total], axis=0), 0.0))
 
-    right = None
+    terms = []
     for n in range(3):
+        at = slice(n * 384, n * 384 + 384)
+        used = slice(0, 64) if n == 0 else slice(64, 96)
         ortho = dot(root, spread[n], (0, 0))
-        ortho_out[:, n * 384 : n * 384 + 384] = ortho
-        term = dot(ortho, merged[n * 384 : n * 384 + 384], (1, 0))
-        right = term if right is None else right + term
-    back_part[...] = right.reshape(CHUNKS, 8, 768)
+        ortho_out[:, at] = ortho
+        ortho_high, ortho_low = halves(ortho[used])
+        size = 64 if n == 0 else 32
+        both = short_dot(jnp.concatenate([ortho_high, ortho_low], axis=0), merged_high[at], (1, 0))
+        terms.append(
+            both[0:size] + both[size : 2 * size] + short_dot(ortho_high, merged_low[at], (1, 0))
+        )
+    back_part[0:8] = terms[0].reshape(8, 8, 768)
+    back_part[8:12] = (terms[1] + terms[2]).reshape(4, 8, 768)
 
     def bpart_copy(d):
         return remote(
@@ -388,6 +410,8 @@
         scratch_shapes=[
             pltpu.VMEM((1152, 768), f32),
             pltpu.VMEM((1152, 768), f32),
+            pltpu.VMEM((1152, 768), jnp.bfloat16),
+            pltpu.VMEM((1152, 768), jnp.bfloat16),
             pltpu.VMEM((96, 768), f32),
             pltpu.VMEM((2, 48, 192), f32),
             pltpu.VMEM((48, 768), f32),
@@ -423,24 +447,36 @@
 
 def update_kernel(
     att_grads, att_errors, ff_grads, ff_errors, ortho, back, base,
-    att_momentum, ff_momentum, att_master, ff_master, small,
+    att_momentum, ff_momentum, att_master, ff_master, small, factor,
     gain_momentum, gain_weight, bias_momentum, bias_weight,
     att_errors_out, ff_errors_out, att_fresh_out, ff_fresh_out,
     att_momentum_out, ff_momentum_out, att_master_out, ff_master_out,
     gain_momentum_out, gain_weight_out, bias_momentum_out, bias_weight_out,
+    att_factor_out, ff_factor_out,
 ):
     n = pl.program_id(0)
     at = pl.ds(pl.multiple_of(n * ROWS, ROWS), ROWS)
-    approx = dot(ortho[:, at], back[...], (0, 0))
-    fresh = (base[...].T - learn_rate * approx).astype(jnp.bfloat16)
+
+    def product(used):
+        left_high, left_low = halves(ortho[used, at])
+        right_high, right_low = halves(back[used])
+        return short_dot(
+            jnp.concatenate([left_high, left_high, left_low], axis=0),
+            jnp.concatenate([right_high, right_low, right_high], axis=0),
+            (0, 0),
+        )
 
     @pl.when(n < 3)
     def _():
+        approx = product(slice(0, 64))
+        fresh = (base[...].T - learn_rate * approx).astype(jnp.bfloat16)
         att_errors_out[...] = att_grads[...] + att_errors[...] - approx
         att_fresh_out[...] = fresh
 
     @pl.when(n >= 3)
     def _():
+        approx = product(slice(64, 96))
+        fresh = (base[...].T - learn_rate * approx).astype(jnp.bfloat16)
         ff_errors_out[...] = ff_grads[...] + ff_errors[...] - approx
         ff_fresh_out[...] = fresh
 
@@ -464,6 +500,8 @@
         bias = decay_rate * bias_momentum[...] + small[1:4, 0:32] * (1.0 / 16.0)
         bias_momentum_out[...] = bias
         bias_weight_out[...] = bias_weight[...] - learn_rate * bias
+        att_factor_out[...] = factor[0:64]
+        ff_factor_out[...] = factor[64:96]
 
 
 def update(*operands):
@@ -487,6 +525,7 @@
         ((2, 48, 192), jnp.float32), ((48, 768), jnp.float32),
         ((1, 192), jnp.float32), ((1, 192), jnp.float32),
         ((3, 32), jnp.float32), ((3, 32), jnp.float32),
+        ((64, 768), jnp.float32), ((32, 768), jnp.float32),
     ]
     return pl.pallas_call(
         update_kernel,
@@ -494,8 +533,9 @@
         out_shape=[jax.ShapeDtypeStruct(*shape) for shape in shapes],
         in_specs=[att, att, ff, ff, whole(96, 1152), whole(96, 768)]
         + [pl.BlockSpec((768, ROWS), lambda n: (0, n))]
-        + states + states + [whole(8, 256)] + vectors,
-        out_specs=[att, ff, att, ff] + states + states + vectors,
+        + states + states + [whole(8, 256), whole(96, 768)] + vectors,
+        out_specs=[att, ff, att, ff] + states + states + vectors
+        + [whole(64, 768), whole(32, 768)],
         name="update",
     )(*operands)
 
@@ -529,21 +569,21 @@
     ortho, back, factor_new, small_total, base_full = exchange(
         att_grads, ff_grads, att_errors, ff_errors,
         jnp.swapaxes(attention_factor, 1, 2).reshape(64, 768), feedforward_factor[0].T,
-        *states, gain_grads.reshape(1, 192), bias_grads.reshape(3, 32),
+        *states, gain_grads.reshape(1, 192), jnp.swapaxes(bias_grads, 0, 1),
     )
     (
         att_errors_new, ff_errors_new, att_fresh, ff_fresh,
         att_momentum_new, ff_momentum_new, att_master_new, ff_master_new, *vectors,
+        att_factor_new, ff_factor_new,
     ) = update(
         att_grads, att_errors, ff_grads, ff_errors, ortho, back, base_full.reshape(768, 1152),
-        *states, small_total, gain_momentum, gain_weight, bias_momentum, bias_weight,
-    )
-    factor_new = jnp.swapaxes(factor_new.reshape(3, 32, 768), 1, 2)
+        *states, small_total, factor_new, gain_momentum, gain_weight, bias_momentum, bias_weight,
+    )
     return (
         att_errors_new.reshape(1, 2, 192, 768),
         ff_errors_new.reshape(1, 1, 768, 768),
-        factor_new[:2],
-        factor_new[2:],
+        jnp.swapaxes(att_factor_new.reshape(2, 32, 768), 1, 2),
+        ff_factor_new.T[None],
         jnp.swapaxes(att_momentum_new, 1, 2),
         ff_momentum_new.T[None],
         jnp.swapaxes(att_master_new, 1, 2),

time: 82.6 us -> 75.2 us (0.910)
  local copies, waits for them, and re-layouts: 4.42 us -> 0 us
  Pallas kernels: 77.2 us -> 74.2 us
    slice x2 -> x0, local copies, waits for them, and re-layouts: 3.16 us -> none  [the longest x1 1.62 us: per_device(): factor_new[:2]]
    pallas_call x1, Pallas kernels: 64.2 us -> 62.6 us  [exchange(): pl.pallas_call(exchange_kernel, out_shape=(jax.ShapeDtypeStruct((96, 1152...]
    pallas_call x1, Pallas kernels: 13 us -> 11.7 us  [update(): pl.pallas_call(update_kernel, grid=(1152 // ROWS,), out_shape=[jax.ShapeD...]
    unnamed x1 -> x0, local copies, waits for them, and re-layouts: 1.26 us -> none
where the time goes in v3:
time: 75.2 us; the launch traced here: 74.9 us
  Pallas kernels  74.2 us (99%)
    pallas_call x1, Pallas kernels, exchange(): pl.pallas_call(exchange_kernel, out_shape=(jax.ShapeDtypeStruct((96, 1152...  62.6 us
    pallas_call x1, Pallas kernels, update(): pl.pallas_call(update_kernel, grid=(1152 // ROWS,), out_shape=[jax.ShapeD...  11.7 us

profile of v3, /device:TPU:0, one launch (start us, length us, event | category | flops | bytes accessed | tf_op | source)
XLA Modules:
  0.0 74.9 jit_solution(13855681391472337151)
XLA Ops:
  0.6 62.6 %exchange.1 = (f32[96,1152]{1,0:T(8,128)}, f32[96,768]{1,0:T(8,128)}, f32[96,768]{1,0:T(8,128)}, f32[8,256]{1,0:T(8,128)}, f32[4,4,2,24,1152]{4,3,2,1,0:T(8,128)}) custom-call(f32[384,768]{1,0:T(8,128)} %bitcast.43, f32[768,768]{1,0:T(8,128)} %bitcast.39, f32[384,768]{1,0:T(8,128)} %bitcast.45, f32[768,768]{1,0:T(8,128)} %bitcast.41, f32[64,768]{1,0:T(8,128)} %bitcast.56, ...), custom_call_target="tpu_custom_call" | custom-call | tf_op jit(solution)/shard_map/exchange/pallas_call | solution.py:399
  63.2 11.7 %update.1 = (f32[384,768]{1,0:T(8,128)}, f32[768,768]{1,0:T(8,128)}, bf16[384,768]{1,0:T(8,128)(2,1)}, bf16[768,768]{1,0:T(8,128)(2,1)}, f32[2,48,192]{2,1,0:T(8...) custom-call(f32[384,768]{1,0:T(8,128)} %bitcast.44, ...), custom_call_target="tpu_custom_call" | custom-call | tf_op jit(solution)/shard_map/update/pallas_call | solution.py:530

commit v4 on v3

--- a/solution.py
+++ b/solution.py
@@ -205,10 +205,6 @@
                 for d in range(1, 4):
                     first_copy(half, d).start()
 
-    @pl.loop(1, 16)
-    def _(d):
-        small_copy(d).start()
-
     def power_copy(d):
         return remote(
             power.at[me], power.at[me], power_send.at[d], power_recv.at[d],
@@ -229,14 +225,6 @@
         @pl.loop(1, 16)
         def _(d):
             power_copy(d).start()
-
-    own_base.wait()
-    for half in range(2):
-        for d in range(1, 4):
-            first_copy(half, d).wait_recv()
-    for half in range(2):
-        for d in range(1, 4):
-            second_copy(half, d).start()
 
     @pl.loop(1, 16)
     def _(d):
@@ -273,6 +261,19 @@
 
     for d in range(1, 4):
         gram_copy(d).start()
+
+    own_base.wait()
+    for half in range(2):
+        for d in range(1, 4):
+            first_copy(half, d).wait_recv()
+    for half in range(2):
+        for d in range(1, 4):
+            second_copy(half, d).start()
+
+    @pl.loop(1, 16)
+    def _(d):
+        small_copy(d).start()
+
     for d in range(1, 4):
         gram_copy(d).wait_recv()
     total = (gram_slots[0] + gram_slots[1]) + (gram_slots[2] + gram_slots[3])
@@ -484,7 +485,13 @@
     def _():
         shard = lax.axis_index("shard")
         own_back = pltpu.roll(back[...], lax.rem(768 - 48 * shard, 768), 1)[:, 0:128]
-        own = dot(own_back, ortho[...], (0, 0))[0:48]
+        left_high, left_low = halves(own_back)
+        right_high, right_low = halves(ortho[...])
+        own = short_dot(
+            jnp.concatenate([left_high, left_high, left_low], axis=0),
+            jnp.concatenate([right_high, right_low, right_high], axis=0),
+            (0, 0),
+        )[0:48]
         step = learn_rate * decay_rate
         att_own = own[:, 0:384]
         for m in range(2):

time: 75.2 us -> 80.7 us (1.073)
  Pallas kernels: 74.2 us -> 79.7 us
    pallas_call x1, Pallas kernels: 62.6 us -> 68.4 us  [exchange(): pl.pallas_call(exchange_kernel, out_shape=(jax.ShapeDtypeStruct((96, 1152...]
where the time goes in v4:
time: 80.7 us; the launch traced here: 80.4 us
  Pallas kernels  79.7 us (99%)
    pallas_call x1, Pallas kernels, exchange(): pl.pallas_call(exchange_kernel, out_shape=(jax.ShapeDtypeStruct((96, 1152...  68.4 us
    pallas_call x1, Pallas kernels, update(): pl.pallas_call(update_kernel, grid=(1152 // ROWS,), out_shape=[jax.ShapeD...  11.4 us

profile of v4, /device:TPU:0, one launch (start us, length us, event | category | flops | bytes accessed | tf_op | source)
XLA Modules:
  0.0 80.4 jit_solution(6530939285422477695)
XLA Ops:
  0.6 68.4 %exchange.1 = (f32[96,1152]{1,0:T(8,128)}, f32[96,768]{1,0:T(8,128)}, f32[96,768]{1,0:T(8,128)}, f32[8,256]{1,0:T(8,128)}, f32[4,4,2,24,1152]{4,3,2,1,0:T(8,128)}) custom-call(f32[384,768]{1,0:T(8,128)} %bitcast.43, f32[768,768]{1,0:T(8,128)} %bitcast.39, f32[384,768]{1,0:T(8,128)} %bitcast.45, f32[768,768]{1,0:T(8,128)} %bitcast.41, f32[64,768]{1,0:T(8,128)} %bitcast.56, ...), custom_call_target="tpu_custom_call" | custom-call | tf_op jit(solution)/shard_map/exchange/pallas_call | solution.py:400
  69.0 11.4 %update.1 = (f32[384,768]{1,0:T(8,128)}, f32[768,768]{1,0:T(8,128)}, bf16[384,768]{1,0:T(8,128)(2,1)}, bf16[768,768]{1,0:T(8,128)(2,1)}, f32[2,48,192]{2,1,0:T(8...) custom-call(f32[384,768]{1,0:T(8,128)} %bitcast.44, ...), custom_call_target="tpu_custom_call" | custom-call | tf_op jit(solution)/shard_map/update/pallas_call | solution.py:537
